TPU v7x, 32 devices: a whole 2x2x4 slice. The times are simulated.
32 devices in a mesh: dp: 4 (over z), expert: 8 (over y, x, core).
Axes of the slice: x: 2, y: 2, z: 4, core: 2. Of those that a mesh axis runs over, the one named last changes fastest.
Arguments:
- act_in: float32 [18912, 768], P(('dp', 'expert')), may hold values from -6 to 6
- w_qkv: float32 [2, 768, 2304], P(None, ('dp', 'expert')), may hold values from -0.21875 to 0.21875
- w_proj: float32 [2, 768, 768], P(None, None, ('dp', 'expert')), may hold values from -1.25 to 1.25
- w_up: float32 [768, 3072], P(('dp', 'expert')), may hold values from -0.21875 to 0.21875
- w_down: float32 [3072, 768], P(None, ('dp', 'expert')), may hold values from -0.109375 to 0.109375
- norm_gain: float32 [4, 768], P(None, ('dp', 'expert')), may hold values from 0.1 to 1.9
- norm_shift: float32 [4, 768], P(None, ('dp', 'expert')), may hold values from -3 to 3
- exp_in: float32 [16, 768, 3072], P('expert', 'dp'), may hold values from -0.21875 to 0.21875
- exp_out: float32 [16, 3072, 768], P('expert', None, 'dp'), may hold values from -0.109375 to 0.109375
- gate: float32 [18912, 2], P(('dp', 'expert')), may hold values from 0.2 to 1
- expert_index: int32 [18912, 2], P(('dp', 'expert')), may hold values from 0 to 15, all different within a row; in each aligned block of 591 rows (0 to 590, 591 to 1181, ...) at most 96 rows name the same one
- cotangent: float32 [18912, 768], P(('dp', 'expert')), may hold values from -6 to 6
Outputs:
- act_out: float32 [18912, 768], P(('dp', 'expert'))
- act_grad: float32 [18912, 768], P(('dp', 'expert'))
- grad_qkv: float32 [2, 768, 2304], P(None, ('dp', 'expert'))
- grad_proj: float32 [2, 768, 768], P(None, None, ('dp', 'expert'))
- grad_up: float32 [768, 3072], P(('dp', 'expert'))
- grad_down: float32 [3072, 768], P(None, ('dp', 'expert'))
- grad_gain: float32 [4, 768], P(None, ('dp', 'expert'))
- grad_shift: float32 [4, 768], P(None, ('dp', 'expert'))
- grad_exp_in: float32 [16, 768, 3072], P('expert', 'dp')
- grad_exp_out: float32 [16, 3072, 768], P('expert', None, 'dp')
- grad_gate: float32 [18912, 2], P(('dp', 'expert'))
Inputs may be any that keep to these rules, and one draw needn't show every extreme that they name: `expert_index`: the 2 entries of a row differ. In each aligned block of 591 rows (the tokens of one device) no expert is named more than 96 times, a bound that some block reaches.
All inputs are finite; a program needn't handle non-finite values.
Results may differ from a plain program's by a relative error of at most 0.018.
The roundings to bfloat16 on the way count: a program that leaves them out, or rounds other values in their place, can miss the bound.
Values may be sent and summed in bfloat16 or wider, within the bound.
No kernel may reach another device: no remote copies, remote signals or barrier semaphores. Data moves between devices by JAX's collectives and lax.ppermute only.
A program may use at most 320 MiB of HBM per device.

v0:
```python
import math
import jax
import jax.numpy as jnp
from jax import lax
from jax.sharding import PartitionSpec as P

D = 768
HEADS = 12
HEAD = 64
SEQ = 197
TOP = 2
EXP_DEV = 2
TOK_DEV = 591


def norm_rows(inputs, gain_row, shift_row):
    average = jnp.mean(inputs, axis=-1, keepdims=True)
    centred = inputs - average
    spread = jnp.mean(centred * centred, axis=-1, keepdims=True)
    return centred * lax.rsqrt(spread + 1e-06) * gain_row + shift_row


def gelu_exact(inputs):
    return jax.nn.gelu(inputs, approximate=False)


def gelu_grad(inputs, upstream):
    _, pull_back = jax.vjp(gelu_exact, inputs)
    return pull_back(upstream)[0]


def norm_grad(inputs, gain_row, shift_row, upstream):
    _, pull_back = jax.vjp(norm_rows, inputs, gain_row, shift_row)
    return pull_back(upstream)


def matmul_low(left, right):
    return jnp.dot(left, right, preferred_element_type=jnp.float32)


def fetch_dense(qkv_part, proj_part, up_part, down_part, gain_part, shift_part):
    fetched = (
        lax.all_gather(qkv_part, ("dp", "expert"), axis=1, tiled=True),
        lax.all_gather(proj_part, ("dp", "expert"), axis=2, tiled=True),
        lax.all_gather(up_part, ("dp", "expert"), axis=0, tiled=True),
        lax.all_gather(down_part, ("dp", "expert"), axis=1, tiled=True),
        lax.all_gather(gain_part, ("dp", "expert"), axis=1, tiled=True),
        lax.all_gather(shift_part, ("dp", "expert"), axis=1, tiled=True),
    )
    return fetched


def reduce_dense(qkv_grad, proj_grad, up_grad, down_grad, gain_grad, shift_grad):
    reduced = (
        lax.psum_scatter(qkv_grad, ("dp", "expert"), scatter_dimension=1, tiled=True),
        lax.psum_scatter(proj_grad, ("dp", "expert"), scatter_dimension=2, tiled=True),
        lax.psum_scatter(up_grad, ("dp", "expert"), scatter_dimension=0, tiled=True),
        lax.psum_scatter(down_grad, ("dp", "expert"), scatter_dimension=1, tiled=True),
        lax.psum_scatter(gain_grad, ("dp", "expert"), scatter_dimension=1, tiled=True),
        lax.psum_scatter(shift_grad, ("dp", "expert"), scatter_dimension=1, tiled=True),
    )
    return reduced


def split_heads(packed_rows):
    images = packed_rows.shape[0] // SEQ
    shaped = packed_rows.reshape(images, SEQ, 3, HEADS, HEAD)
    return (shaped[:, :, 0], shaped[:, :, 1], shaped[:, :, 2])


def attend_forward(normed_low, qkv_weight, proj_weight):
    score_scale = 1.0 / math.sqrt(HEAD)
    packed = matmul_low(normed_low, qkv_weight).astype(jnp.bfloat16)
    query_rows, key_rows, value_rows = split_heads(packed)
    scores = (
        jnp.einsum("bqhd,bkhd->bhqk", query_rows, key_rows, preferred_element_type=jnp.float32)
        * score_scale
    )
    row_peak = jnp.max(scores, axis=-1, keepdims=True)
    raised = jnp.exp(scores - row_peak)
    row_total = jnp.sum(raised, axis=-1, keepdims=True)
    attn_weights = raised / row_total
    log_total = row_peak + jnp.log(row_total)
    mixed_rows = jnp.einsum(
        "bhqk,bkhd->bqhd",
        attn_weights.astype(jnp.bfloat16),
        value_rows,
        preferred_element_type=jnp.float32,
    )
    mixed_rows = mixed_rows.astype(jnp.bfloat16).reshape(packed.shape[0], D)
    branch = matmul_low(mixed_rows, proj_weight)
    return (branch, (packed, log_total, mixed_rows))


def attend_backward(grad_branch, normed_low, qkv_weight, proj_weight, saved):
    score_scale = 1.0 / math.sqrt(HEAD)
    packed, log_total, mixed_rows = saved
    row_count = packed.shape[0]
    grad_low = grad_branch.astype(jnp.bfloat16)
    grad_proj = jnp.einsum("td,te->de", mixed_rows, grad_low, preferred_element_type=jnp.float32)
    grad_mixed = jnp.einsum("te,de->td", grad_low, proj_weight, preferred_element_type=jnp.float32)
    grad_mixed = grad_mixed.astype(jnp.bfloat16).reshape(row_count // SEQ, SEQ, HEADS, HEAD)
    query_rows, key_rows, value_rows = split_heads(packed)
    scores = (
        jnp.einsum("bqhd,bkhd->bhqk", query_rows, key_rows, preferred_element_type=jnp.float32)
        * score_scale
    )
    attn_weights = jnp.exp(scores - log_total)
    grad_weights = jnp.einsum(
        "bqhd,bkhd->bhqk", grad_mixed, value_rows, preferred_element_type=jnp.float32
    )
    grad_values = jnp.einsum(
        "bhqk,bqhd->bkhd",
        attn_weights.astype(jnp.bfloat16),
        grad_mixed,
        preferred_element_type=jnp.float32,
    )
    grad_scores = attn_weights * (
        grad_weights - jnp.sum(attn_weights * grad_weights, axis=-1, keepdims=True)
    )
    grad_scores = grad_scores.astype(jnp.bfloat16)
    grad_query = (
        jnp.einsum("bhqk,bkhd->bqhd", grad_scores, key_rows, preferred_element_type=jnp.float32)
        * score_scale
    )
    grad_keys = (
        jnp.einsum("bhqk,bqhd->bkhd", grad_scores, query_rows, preferred_element_type=jnp.float32)
        * score_scale
    )
    grad_packed = (
        jnp.stack([grad_query, grad_keys, grad_values], axis=2)
        .reshape(row_count, 3 * D)
        .astype(jnp.bfloat16)
    )
    grad_qkv = jnp.einsum("td,tf->df", normed_low, grad_packed, preferred_element_type=jnp.float32)
    grad_normed = jnp.einsum(
        "tf,df->td", grad_packed, qkv_weight, preferred_element_type=jnp.float32
    )
    return (grad_normed, grad_qkv, grad_proj)


def local(
    act_in,
    w_qkv,
    w_proj,
    w_up,
    w_down,
    norm_gain,
    norm_shift,
    exp_in,
    exp_out,
    gate,
    expert_index,
    cotangent,
):
    row_count = act_in.shape[0]
    experts_all = EXP_DEV * lax.axis_size("expert")
    capacity = (TOP * TOK_DEV * 5 // (4 * experts_all) + 7) // 8 * 8
    dense_low = fetch_dense(
        w_qkv.astype(jnp.bfloat16),
        w_proj.astype(jnp.bfloat16),
        w_up.astype(jnp.bfloat16),
        w_down.astype(jnp.bfloat16),
        norm_gain.astype(jnp.bfloat16),
        norm_shift.astype(jnp.bfloat16),
    )
    qkv_all, proj_all, up_all, down_all, gain_all, shift_all = dense_low
    gain_full = gain_all.astype(jnp.float32)
    shift_full = shift_all.astype(jnp.float32)
    expert_low = (
        lax.all_gather(exp_in.astype(jnp.bfloat16), "dp", axis=1, tiled=True),
        lax.all_gather(exp_out.astype(jnp.bfloat16), "dp", axis=2, tiled=True),
    )
    exp_in_all, exp_out_all = expert_low
    normed_a = norm_rows(act_in, gain_full[0], shift_full[0]).astype(jnp.bfloat16)
    branch_a, saved_a = attend_forward(normed_a, qkv_all[0], proj_all[0])
    after_a = act_in + branch_a
    normed_b = norm_rows(after_a, gain_full[1], shift_full[1]).astype(jnp.bfloat16)
    inner_rows = matmul_low(normed_b, up_all)
    hidden_low = gelu_exact(inner_rows).astype(jnp.bfloat16)
    after_b = after_a + matmul_low(hidden_low, down_all)
    normed_c = norm_rows(after_b, gain_full[2], shift_full[2]).astype(jnp.bfloat16)
    branch_c, saved_c = attend_forward(normed_c, qkv_all[1], proj_all[1])
    after_c = after_b + branch_c
    sent_low = norm_rows(after_c, gain_full[3], shift_full[3]).astype(jnp.bfloat16)
    flat_index = expert_index.reshape(-1)
    onehot = (flat_index[:, None] == jnp.arange(experts_all, dtype=jnp.int32)[None, :]).astype(
        jnp.int32
    )
    before = jnp.cumsum(onehot, axis=0) - onehot
    places = flat_index * capacity + jnp.sum(onehot * before, axis=1)
    repeated = jnp.repeat(sent_low, TOP, axis=0)
    send_buffer = (
        jnp.zeros((experts_all * capacity, D), jnp.bfloat16)
        .at[places]
        .set(repeated)
        .reshape(experts_all, capacity, D)
    )
    arrived = lax.all_to_all(send_buffer, "expert", split_axis=0, concat_axis=1, tiled=True)
    expert_inner = jnp.einsum(
        "erd,edf->erf", arrived, exp_in_all, preferred_element_type=jnp.float32
    )
    expert_hidden = gelu_exact(expert_inner).astype(jnp.bfloat16)
    expert_result = jnp.einsum(
        "erf,efd->erd", expert_hidden, exp_out_all, preferred_element_type=jnp.float32
    ).astype(jnp.bfloat16)
    returned = lax.all_to_all(expert_result, "expert", split_axis=1, concat_axis=0, tiled=True)
    picked = returned.reshape(-1, D)[places].astype(jnp.float32).reshape(row_count, TOP, D)
    act_out = after_c + jnp.sum(gate[:, :, None] * picked, axis=1)
    dense_back = fetch_dense(
        w_qkv.astype(jnp.bfloat16),
        w_proj.astype(jnp.bfloat16),
        w_up.astype(jnp.bfloat16),
        w_down.astype(jnp.bfloat16),
        norm_gain.astype(jnp.bfloat16),
        norm_shift.astype(jnp.bfloat16),
    )
    qkv_back, proj_back, up_back, down_back, gain_back, shift_back = dense_back
    gain_bf = gain_back.astype(jnp.float32)
    shift_bf = shift_back.astype(jnp.float32)
    grad_gate = jnp.sum(cotangent[:, None, :] * picked, axis=2)
    grad_slots = (
        (gate[:, :, None] * cotangent[:, None, :]).astype(jnp.bfloat16).reshape(row_count * TOP, D)
    )
    grad_buffer = (
        jnp.zeros((experts_all * capacity, D), jnp.bfloat16)
        .at[places]
        .set(grad_slots)
        .reshape(experts_all, capacity, D)
    )
    grad_arrived = lax.all_to_all(grad_buffer, "expert", split_axis=0, concat_axis=1, tiled=True)
    local_exp_out = jnp.einsum(
        "erf,erd->efd", expert_hidden, grad_arrived, preferred_element_type=jnp.float32
    )
    grad_hidden = jnp.einsum(
        "erd,efd->erf", grad_arrived, exp_out_all, preferred_element_type=jnp.float32
    )
    grad_inner = gelu_grad(expert_inner, grad_hidden).astype(jnp.bfloat16)
    local_exp_in = jnp.einsum(
        "erd,erf->edf", arrived, grad_inner, preferred_element_type=jnp.float32
    )
    grad_routed = jnp.einsum(
        "erf,edf->erd", grad_inner, exp_in_all, preferred_element_type=jnp.float32
    ).astype(jnp.bfloat16)
    grad_home = lax.all_to_all(grad_routed, "expert", split_axis=1, concat_axis=0, tiled=True)
    grad_sent = jnp.sum(
        grad_home.reshape(-1, D)[places].astype(jnp.float32).reshape(row_count, TOP, D), axis=1
    )
    grad_exp_in, grad_exp_out = (
        lax.psum_scatter(
            local_exp_in.astype(jnp.bfloat16), "dp", scatter_dimension=1, tiled=True
        ).astype(jnp.float32),
        lax.psum_scatter(
            local_exp_out.astype(jnp.bfloat16), "dp", scatter_dimension=2, tiled=True
        ).astype(jnp.float32),
    )
    grad_after_c, gain_d, shift_d = norm_grad(after_c, gain_bf[3], shift_bf[3], grad_sent)
    grad_after_c = cotangent + grad_after_c
    grad_normed_c, qkv_grad_c, proj_grad_c = attend_backward(
        grad_after_c, normed_c, qkv_back[1], proj_back[1], saved_c
    )
    through_c, gain_c, shift_c = norm_grad(after_b, gain_bf[2], shift_bf[2], grad_normed_c)
    grad_after_b = grad_after_c + through_c
    grad_mlp = grad_after_b.astype(jnp.bfloat16)
    down_grad = jnp.einsum("tf,td->fd", hidden_low, grad_mlp, preferred_element_type=jnp.float32)
    grad_hidden_b = jnp.einsum("td,fd->tf", grad_mlp, down_back, preferred_element_type=jnp.float32)
    grad_inner_b = gelu_grad(inner_rows, grad_hidden_b).astype(jnp.bfloat16)
    up_grad = jnp.einsum("td,tf->df", normed_b, grad_inner_b, preferred_element_type=jnp.float32)
    grad_normed_b = jnp.einsum(
        "tf,df->td", grad_inner_b, up_back, preferred_element_type=jnp.float32
    )
    through_b, gain_b, shift_b = norm_grad(after_a, gain_bf[1], shift_bf[1], grad_normed_b)
    grad_after_a = grad_after_b + through_b
    grad_normed_a, qkv_grad_a, proj_grad_a = attend_backward(
        grad_after_a, normed_a, qkv_back[0], proj_back[0], saved_a
    )
    through_a, gain_a, shift_a = norm_grad(act_in, gain_bf[0], shift_bf[0], grad_normed_a)
    act_grad = grad_after_a + through_a
    reduced = reduce_dense(
        jnp.stack([qkv_grad_a, qkv_grad_c]),
        jnp.stack([proj_grad_a, proj_grad_c]),
        up_grad,
        down_grad,
        jnp.stack([gain_a, gain_b, gain_c, gain_d]),
        jnp.stack([shift_a, shift_b, shift_c, shift_d]),
    )
    return (
        act_out,
        act_grad,
        reduced[0],
        reduced[1],
        reduced[2],
        reduced[3],
        reduced[4],
        reduced[5],
        grad_exp_in,
        grad_exp_out,
        grad_gate,
    )


def solution(mesh):
    in_specs = (
        P(("dp", "expert"), None),
        P(None, ("dp", "expert"), None),
        P(None, None, ("dp", "expert")),
        P(("dp", "expert"), None),
        P(None, ("dp", "expert")),
        P(None, ("dp", "expert")),
        P(None, ("dp", "expert")),
        P("expert", "dp", None),
        P("expert", None, "dp"),
        P(("dp", "expert"), None),
        P(("dp", "expert"), None),
        P(("dp", "expert"), None),
    )
    out_specs = (
        P(("dp", "expert"), None),
        P(("dp", "expert"), None),
        P(None, ("dp", "expert"), None),
        P(None, None, ("dp", "expert")),
        P(("dp", "expert"), None),
        P(None, ("dp", "expert")),
        P(None, ("dp", "expert")),
        P(None, ("dp", "expert")),
        P("expert", "dp", None),
        P("expert", None, "dp"),
        P(("dp", "expert"), None),
    )
    return jax.shard_map(local, mesh=mesh, in_specs=in_specs, out_specs=out_specs, check_vma=False)
```

profile of v0, /device:TPU:0, one launch (start us, length us, event | category | flops | bytes accessed | tf_op | source)
XLA Modules:
  0.0 1840.9 jit_solution(3664145385643357674)
XLA Ops:
  33.4 15.2 scatter_custom_fusion.1
  59.2 69.3 %all-gather.1 = bf16[32,24,4]{1,2,0:T(4,128)(2,1)S(1)} all-gather(bf16[1,24,4]{1,2,0:T(4,128)(2,1)S(1)} %convert_bitcast_fusion), channel_id=1, replica_groups=mesh['dp'=4,'expert'=8] {'dp','expert'}, dimensions={0}, use_global_device_ids=true | all-gather | bytes 6336 | tf_op jit(solution)/shard_map/all_gather | solution.py:48
  128.7 37.0 %all-gather = bf16[32,24,4]{1,2,0:T(4,128)(2,1)S(1)} all-gather(bf16[1,24,4]{1,2,0:T(4,128)(2,1)S(1)} %convert_bitcast_fusion.1), channel_id=1, replica_groups=mesh['dp'=4,'expert'=8] {'dp','expert'}, dimensions={0}, use_global_device_ids=true | all-gather | bytes 6336 | tf_op jit(solution)/shard_map/all_gather | solution.py:47
  172.3 9.3 reshape.365
  217.4 15.5 all-gather.13.cloned.1.call-done
  232.9 35.6 %multiply_convert_fusion.3 = (bf16[591,3072]{1,0:T(8,128)(2,1)}, f32[591,3072]{1,0:T(8,128)}, f32[591,3072]{1,0:T(8,128)}) fusion(bf16[768,3072]{1,0:T(8,128)(2,1)} %all-gather.13.cloned.1.call-done, f32[591,768]{1,0:T(8,128)} %copy-done.6, f32[768]{0:T(1024)S(1)} %get-tuple-element.76, f32[768]{0:T(1024)S(1)} %get-tuple-element.119, f32[591]{0:T(1024)S(1)} %fusion.75, ...), kind=kOutput, calls=%fused_computation.39 | convolution fusion | flops 2908968192 | bytes 24700536 | tf_op jit(solution)/shard_map/dot_general | solution.py:38
  268.5 30.2 %all-gather.15.cloned.1.call-done = bf16[3072,768]{0,1:T(8,128)(2,1)} async-done(((bf16[3072,24]{0,1:T(8,128)(2,1)}), bf16[3072,768]{0,1:T(8,128)(2,1)}) %all-gather.15.cloned.1.call-update) | async-done | bytes 4718608 | tf_op jit(solution)/shard_map/all_gather | solution.py:46
  356.5 10.4 scatter_custom_fusion
  373.9 26.1 %all-to-all-done = bf16[16,96,768]{2,1,0:T(8,128)(2,1)S(1)} async-done(((bf16[16,96,768]{2,1,0:T(8,128)(2,1)}), bf16[16,96,768]{2,1,0:T(8,128)(2,1)S(1)}, u32[]{:S(2)}, u32[]{:S(2)}) %all-to-all-start) | async-done | bytes 2359328 | tf_op jit(solution)/shard_map/all_to_all | solution.py:199
  401.5 64.2 %all-gather.17.cloned.1.call-done = bf16[2,768,3072]{2,1,0:T(8,128)(2,1)} async-done(((bf16[2,192,3072]{2,1,0:T(8,128)(2,1)}), bf16[2,768,3072]{2,1,0:T(8,128)(2,1)}) %all-gather.17.cloned.1.call-update) | async-done | bytes 9437200 | tf_op jit(solution)/shard_map/all_gather | solution.py:171
  465.8 22.8 %fusion.17 = (u8[768,3072]{1,0:T(8,128)(4,1)}, u8[768,3072]{1,0:T(8,128)(4,1)}, f32[2,768,3072]{2,1,0:T(8,128)}) fusion(bf16[2,768,768]{2,1,0:T(8,128)(2,1)} %bitcast.200, bf16[2,768,3072]{2,1,0:T(8,128)(2,1)} %all-gather.17.cloned.1.call-done), kind=kOutput, calls=%fused_computation.67 | convolution fusion | flops 7304380416 | bytes 35389440 | tf_op jit(solution)/shard_map/erd,edf->erf/dot_general | solution.py:200
  488.6 143.6 %all-gather.19.cloned.1.call-done = bf16[2,3072,768]{1,2,0:T(8,128)(2,1)} async-done(((bf16[2,3072,192]{1,2,0:T(8,128)(2,1)}), bf16[2,3072,768]{1,2,0:T(8,128)(2,1)}) %all-gather.19.cloned.1.call-update) | async-done | bytes 9437200 | tf_op jit(solution)/shard_map/all_gather | solution.py:172
  632.2 56.1 %add_convert_fusion = (bf16[2,768,3072]{2,1,0:T(8,128)(2,1)}, f32[2,768,3072]{2,1,0:T(8,128)}) fusion(f32[2,768,3072]{2,1,0:T(8,128)} %get-tuple-element.110, u8[768,3072]{1,0:T(8,128)(4,1)} %get-tuple-element.56, u8[768,3072]{1,0:T(8,128)(4,1)} %get-tuple-element.55, bf16[2,768,768]{2,1,0:T(8,128)(2,1)S(1)} %bitcast.203, ...), kind=kOutput, calls=%fused_computation.11 | convolution fusion | flops 7611088896 | bytes 63700992 | tf_op jit(solution)/shard_map/erd,efd->erf/dot_general | solution.py:235
  688.3 13.2 multiply_convert_fusion
  701.5 10.1 convolution_convert_fusion.4
  719.5 12.9 convolution_convert_fusion.5
  736.3 12.7 all-to-all-done.3
  755.5 27.3 %all-to-all-done.1 = bf16[2,768,768]{2,0,1:T(2,128)(2,1)} async-done(((bf16[2,768,768]{2,0,1:T(2,128)(2,1)}), bf16[2,768,768]{2,0,1:T(2,128)(2,1)}, u32[]{:S(2)}, u32[]{:S(2)}) %all-to-all-start.1) | async-done | bytes 2359328 | tf_op jit(solution)/shard_map/all_to_all | solution.py:207
  804.0 10.9 multiply_reduce_fusion.4
  864.0 10.0 convert_element_type.222
  883.1 9.5 add_convert_fusion.1
  910.7 13.7 convolution_convert_fusion
  924.5 14.4 convolution_convert_fusion.1
  988.1 10.1 convert_element_type.230
  998.3 8.7 convolution_bitcast_fusion
  1012.6 11.3 pad_maximum_fusion
  1033.8 37.3 %all-reduce.4 = (f32[4,768]{1,0:T(4,128)S(1)}, f32[4,768]{1,0:T(4,128)S(1)}) all-reduce(f32[4,768]{1,0:T(4,128)S(1)} %pad_maximum_fusion.2, f32[4,768]{1,0:T(4,128)S(1)} %pad_maximum_fusion.3), channel_id=6, replica_groups=mesh['dp'=4,'expert'=8] {'dp','expert'}, use_global_device_ids=true, to_apply=%region_37.38.clone | all-reduce | flops 6144 | bytes 49152
  1077.7 137.2 %reduce-scatter.16.cloned.1.call-done = bf16[2,3072,192]{1,2,0:T(8,128)(2,1)} async-done(((bf16[2,3072,768]{1,2,0:T(8,128)(2,1)}), bf16[2,3072,192]{1,2,0:T(8,128)(2,1)}) %reduce-scatter.16.cloned.1.call-update) | async-done | bytes 2359312 | tf_op jit(solution)/shard_map/reduce_scatter | solution.py:253
  1219.3 160.2 %reduce-scatter.14.cloned.1.call-done = bf16[2,192,3072]{2,1,0:T(8,128)(2,1)} async-done(((bf16[2,768,3072]{2,1,0:T(8,128)(2,1)}), bf16[2,192,3072]{2,1,0:T(8,128)(2,1)}) %reduce-scatter.14.cloned.1.call-update) | async-done | bytes 2359312 | tf_op jit(solution)/shard_map/reduce_scatter | solution.py:250
  1384.0 139.3 %reduce-scatter.10.cloned.1.call-done = f32[24,3072]{1,0:T(8,128)} async-done(((f32[768,3072]{1,0:T(8,128)}), f32[24,3072]{1,0:T(8,128)}) %reduce-scatter.10.cloned.1.call-update) | async-done | bytes 294928 | tf_op jit(solution)/shard_map/reduce_scatter | solution.py:57
  1523.3 141.3 %reduce-scatter.12.cloned.1.call-done = f32[3072,24]{0,1:T(8,128)} async-done(((f32[3072,768]{0,1:T(8,128)}), f32[3072,24]{0,1:T(8,128)}) %reduce-scatter.12.cloned.1.call-update) | async-done | bytes 294928 | tf_op jit(solution)/shard_map/reduce_scatter | solution.py:58
  1664.6 169.1 %reduce-scatter.8.cloned.1.call-done = f32[2,24,2304]{2,1,0:T(8,128)} async-done(((f32[2,768,2304]{2,1,0:T(8,128)}), f32[2,24,2304]{2,1,0:T(8,128)}) %reduce-scatter.8.cloned.1.call-update) | async-done | bytes 442384 | tf_op jit(solution)/shard_map/reduce_scatter | solution.py:55
  (413 shorter events, 340.3 us)
Async XLA Ops:
  7.2 159.2 %all-gather.9.cloned.1.call-start = ((), (), s32[]{:S(2)}) async-start(), calls=%async_computation.9 | async-start | bytes 7299072 | tf_op jit(solution)/shard_map/all_gather | solution.py:43
  9.0 204.1 %all-gather.11.cloned.1.call-start = ((), (), s32[]{:S(2)}) async-start(), calls=%async_computation.10 | async-start | bytes 2433024 | tf_op jit(solution)/shard_map/all_gather | solution.py:44
  10.6 222.3 %all-gather.13.cloned.1.call-start = ((), (), s32[]{:S(2)}) async-start(), calls=%async_computation.11 | async-start | bytes 4866048 | tf_op jit(solution)/shard_map/all_gather | solution.py:45
  12.3 286.4 %all-gather.15.cloned.1.call-start = ((), (), s32[]{:S(2)}) async-start(), calls=%async_computation.12 | async-start | bytes 4866048 | tf_op jit(solution)/shard_map/all_gather | solution.py:46
  14.1 451.7 %all-gather.17.cloned.1.call-start = ((), (), s32[]{:S(2)}) async-start(), calls=%async_computation.13 | async-start | bytes 11796480 | tf_op jit(solution)/shard_map/all_gather | solution.py:171
  33.3 323.1 %copy-start.84 = (s32[1182]{0:T(1024)}, s32[1182]{0:T(1024)S(1)}, u32[]{:S(2)}) copy-start(s32[1182]{0:T(1024)S(1)} %fusion.73) | copy-start | bytes 14188
  48.5 318.3 %all-to-all-start.2 = ((bf16[16,96,768]{2,1,0:T(8,128)(2,1)}), bf16[16,96,768]{2,1,0:T(8,128)(2,1)}, u32[]{:S(2)}, u32[]{:S(2)}) async-start(bf16[16,96,768]{2,1,0:T(8,128)(2,1)} %bitcast.26), calls=%async_computation.2 | async-start | bytes 4718592 | tf_op jit(solution)/shard_map/all_to_all | solution.py:231
  53.7 578.5 %all-gather.19.cloned.1.call-start = ((), (), s32[]{:S(2)}) async-start(), calls=%async_computation.14 | async-start | bytes 11796480 | tf_op jit(solution)/shard_map/all_gather | solution.py:172
  58.3 114.0 %copy-start.72 = (f32[591]{0:T(1024)}, f32[591]{0:T(1024)S(1)}, u32[]{:S(2)}) copy-start(f32[591]{0:T(1024)S(1)} %broadcast_multiply_fusion.4) | copy-start | bytes 7096
  59.2 113.1 %copy-start.91 = (f32[591]{0:T(1024)}, f32[591]{0:T(1024)S(1)}, u32[]{:S(2)}) copy-start(f32[591]{0:T(1024)S(1)} %fusion.74) | copy-start | bytes 7096
  166.3 66.6 %copy-start.56 = (f32[768]{0:T(1024)}, f32[768]{0:T(1024)S(1)}, u32[]{:S(2)}) copy-start(f32[768]{0:T(1024)S(1)} %get-tuple-element.119) | copy-start | bytes 9220
  166.3 66.6 %copy-start.60 = (f32[768]{0:T(1024)}, f32[768]{0:T(1024)S(1)}, u32[]{:S(2)}) copy-start(f32[768]{0:T(1024)S(1)} %get-tuple-element.76) | copy-start | bytes 9220
  166.3 139.4 %copy-start.89 = (f32[768]{0:T(1024)}, f32[768]{0:T(1024)S(1)}, u32[]{:S(2)}) copy-start(f32[768]{0:T(1024)S(1)} %get-tuple-element.120) | copy-start | bytes 9220
  166.3 139.4 %copy-start.99 = (f32[768]{0:T(1024)}, f32[768]{0:T(1024)S(1)}, u32[]{:S(2)}) copy-start(f32[768]{0:T(1024)S(1)} %get-tuple-element.75) | copy-start | bytes 9220
  166.3 184.1 %copy-start.68 = (f32[768]{0:T(1024)}, f32[768]{0:T(1024)S(1)}, u32[]{:S(2)}) copy-start(f32[768]{0:T(1024)S(1)} %get-tuple-element.121) | copy-start | bytes 9220
  215.8 52.7 %copy-start.54 = (f32[591]{0:T(1024)}, f32[591]{0:T(1024)S(1)}, u32[]{:S(2)}) copy-start(f32[591]{0:T(1024)S(1)} %broadcast_multiply_fusion.3) | copy-start | bytes 7096
  217.4 51.1 %copy-start.78 = (f32[591]{0:T(1024)}, f32[591]{0:T(1024)S(1)}, u32[]{:S(2)}) copy-start(f32[591]{0:T(1024)S(1)} %multiply_reduce_fusion.16) | copy-start | bytes 7096
  217.4 51.1 %copy-start.58 = (f32[591]{0:T(1024)}, f32[591]{0:T(1024)S(1)}, u32[]{:S(2)}) copy-start(f32[591]{0:T(1024)S(1)} %fusion.75) | copy-start | bytes 7096
  232.9 65.8 %copy-start.7 = (f32[591,768]{1,0:T(8,128)S(1)}, f32[591,768]{1,0:T(8,128)}, u32[]{:S(2)}) copy-start(f32[591,768]{1,0:T(8,128)} %copy-done.6) | copy-start | bytes 5446660
  366.8 33.2 %all-to-all-start = ((bf16[16,96,768]{2,1,0:T(8,128)(2,1)}), bf16[16,96,768]{2,1,0:T(8,128)(2,1)S(1)}, u32[]{:S(2)}, u32[]{:S(2)}) async-start(bf16[16,96,768]{2,1,0:T(8,128)(2,1)} %bitcast.19), calls=%async_computation | async-start | bytes 4718592 | tf_op jit(solution)/shard_map/all_to_all | solution.py:199
  465.8 166.4 %copy-start.48 = (bf16[2,8,96,768]{3,2,1,0:T(8,128)(2,1)S(1)}, bf16[2,8,96,768]{3,2,1,0:T(8,128)(2,1)}, u32[]{:S(2)}) copy-start(bf16[2,8,96,768]{3,2,1,0:T(8,128)(2,1)} %copy.152) | copy-start | bytes 7077892
  632.2 56.1 %copy-start.9 = (f32[2,768,3072]{2,1,0:T(8,128)S(1)}, f32[2,768,3072]{2,1,0:T(8,128)}, u32[]{:S(2)}) copy-start(f32[2,768,3072]{2,1,0:T(8,128)} %get-tuple-element.110) | copy-start | bytes 56623108
  715.4 33.5 %all-to-all-start.3 = ((bf16[2,768,768]{2,0,1:T(2,128)(2,1)}), bf16[2,768,768]{2,0,1:T(2,128)(2,1)S(1)}, u32[]{:S(2)}, u32[]{:S(2)}) async-start(bf16[2,768,768]{2,0,1:T(2,128)(2,1)} %copy.153), calls=%async_computation.3 | async-start | bytes 4718592 | tf_op jit(solution)/shard_map/all_to_all | solution.py:245
  732.4 21.0 %copy-start.53 = (f32[3,12,197]{2,1,0:T(8,128)S(1)}, f32[3,12,197]{2,1,0:T(8,128)}, u32[]{:S(2)}) copy-start(f32[3,12,197]{2,1,0:T(8,128)} %copy-done.52) | copy-start | bytes 85108
  748.9 33.9 %all-to-all-start.1 = ((bf16[2,768,768]{2,0,1:T(2,128)(2,1)}), bf16[2,768,768]{2,0,1:T(2,128)(2,1)}, u32[]{:S(2)}, u32[]{:S(2)}) async-start(bf16[2,768,768]{2,0,1:T(2,128)(2,1)} %copy.149), calls=%async_computation.1 | async-start | bytes 4718592 | tf_op jit(solution)/shard_map/all_to_all | solution.py:207
  753.3 322.8 %all-reduce.7.cloned.1.call-start = ((), (), s32[]{:S(2)}) async-start(), calls=%async_computation.20 | async-start | bytes 9437184
  910.7 304.3 %reduce-scatter.16.cloned.1.call-start = ((), (), s32[]{:S(2)}) async-start(), calls=%async_computation.19 | async-start | bytes 11796480 | tf_op jit(solution)/shard_map/reduce_scatter | solution.py:253
  924.5 455.1 %reduce-scatter.14.cloned.1.call-start = ((), (), s32[]{:S(2)}) async-start(), calls=%async_computation.18 | async-start | bytes 11796480 | tf_op jit(solution)/shard_map/reduce_scatter | solution.py:250
  939.0 584.3 %reduce-scatter.10.cloned.1.call-start = ((), (), s32[]{:S(2)}) async-start(), calls=%async_computation.16 | async-start | bytes 9732096 | tf_op jit(solution)/shard_map/reduce_scatter | solution.py:57
  948.2 716.3 %reduce-scatter.12.cloned.1.call-start = ((), (), s32[]{:S(2)}) async-start(), calls=%async_computation.17 | async-start | bytes 9732096 | tf_op jit(solution)/shard_map/reduce_scatter | solution.py:58
  958.0 875.6 %reduce-scatter.8.cloned.1.call-start = ((), (), s32[]{:S(2)}) async-start(), calls=%async_computation.15 | async-start | bytes 14598144 | tf_op jit(solution)/shard_map/reduce_scatter | solution.py:55
  1026.7 45.8 %copy-start.77 = (f32[591]{0:T(1024)S(1)}, f32[591]{0:T(1024)}, u32[]{:S(2)}) copy-start(f32[591]{0:T(1024)} %copy-done.76) | copy-start | bytes 7096
  (96 other events, 525.3 us)
Sparse Core Ops, SparseCore 0:
  11.5 89.3 all-gather.8
  104.4 62.3 all-gather.10
  170.3 62.5 all-gather.12
  236.2 62.4 all-gather.14
  300.1 165.5 all-gather.16
  467.2 164.9 all-gather.18
  910.8 141.2 all-reduce.6
  1054.5 160.3 reduce-scatter.15
  1217.4 162.1 reduce-scatter.13
  1386.9 136.3 reduce-scatter.9
  1529.7 134.7 reduce-scatter.11
  1672.0 161.5 reduce-scatter.7
where the time goes:
time: 1850 us; the launch traced here: 1840 us
  waiting for transfers between devices  1070 us (58%)
  matrix products  279 us (15%)
  local copies, waits for them, and re-layouts  204 us (11%)
  blocking collectives  144 us (8%)
  other arithmetic  114 us (6%)
    reduce_scatter x1, waiting for transfers between devices, reduce_dense(): lax.psum_scatter(qkv_grad, ('dp', 'expert'), scatter_dimension=1, tiled=T...  169 us
    reduce_scatter x1, waiting for transfers between devices, local(): lax.psum_scatter(local_exp_in.astype(jnp.bfloat16), 'dp', scatter_dimensi...  160 us
    all_gather x1, waiting for transfers between devices, local(): lax.all_gather(exp_out.astype(jnp.bfloat16), 'dp', axis=2, tiled=True)  144 us
    reduce_scatter x1, waiting for transfers between devices, reduce_dense(): lax.psum_scatter(down_grad, ('dp', 'expert'), scatter_dimension=1, tiled=...  141 us
    reduce_scatter x1, waiting for transfers between devices, reduce_dense(): lax.psum_scatter(up_grad, ('dp', 'expert'), scatter_dimension=0, tiled=True)  139 us
    reduce_scatter x1, waiting for transfers between devices, local(): lax.psum_scatter(local_exp_out.astype(jnp.bfloat16), 'dp', scatter_dimens...  137 us
    all_gather x1, blocking collectives, fetch_dense(): lax.all_gather(shift_part, ('dp', 'expert'), axis=1, tiled=True)  69.3 us
    all_gather x1, waiting for transfers between devices, local(): lax.all_gather(exp_in.astype(jnp.bfloat16), 'dp', axis=1, tiled=True)  64.2 us
  transfers between devices with their start and end apart: 16, of which 12 were waited for; matrix products, arithmetic and copies ran while one was open for 20% of the time, Pallas kernels for 0%

commit v1 on v0

--- a/solution.py
+++ b/solution.py
@@ -13,6 +13,18 @@
 TOK_DEV = 591
 
 
+def doubled_up(value, axis, dim):
+    ways, here, step = (lax.axis_size(axis), lax.axis_index(axis), value.shape[dim])
+    line, have = (value, 1)
+    while have < ways:
+        line = jnp.concatenate(
+            [line, lax.ppermute(line, axis, [(d, (d - have) % ways) for d in range(ways)])],
+            axis=dim,
+        )
+        have = 2 * have
+    return jnp.roll(line, here * step, axis=dim)
+
+
 def norm_rows(inputs, gain_row, shift_row):
     average = jnp.mean(inputs, axis=-1, keepdims=True)
     centred = inputs - average
@@ -45,7 +57,7 @@
         lax.all_gather(up_part, ("dp", "expert"), axis=0, tiled=True),
         lax.all_gather(down_part, ("dp", "expert"), axis=1, tiled=True),
         lax.all_gather(gain_part, ("dp", "expert"), axis=1, tiled=True),
-        lax.all_gather(shift_part, ("dp", "expert"), axis=1, tiled=True),
+        doubled_up(shift_part, ("dp", "expert"), 1),
     )
     return fetched
 

time: 1850 us -> 1860 us (level)
  blocking collectives: 144 us -> 79.5 us
  waiting for transfers between devices: 1070 us -> 1120 us
    all_gather x1 -> x0, blocking collectives: 69.3 us -> none  [fetch_dense(): lax.all_gather(shift_part, ('dp', 'expert'), axis=1, tiled=True)]
    ppermute x0 -> x5, waiting for transfers between devices: none -> 38.7 us  [doubled_up(): lax.ppermute(line, axis, [(d, (d - have) % ways) for d in range(ways)])]
    all_gather x1, waiting for transfers between devices: 15.5 us -> 34.5 us  [fetch_dense(): lax.all_gather(up_part, ('dp', 'expert'), axis=0, tiled=True)]
  transfers between devices with their start and end apart: 16 -> 21, of which waited for: 12 -> 15; matrix products, arithmetic and copies ran while one was open for 20% -> 20% of each run, Pallas kernels for 0% -> 0%
where the time goes in v1:
time: 1860 us; the launch traced here: 1840 us
  waiting for transfers between devices  1120 us (60%)
  matrix products  279 us (15%)
  local copies, waits for them, and re-layouts  203 us (11%)
  other arithmetic  115 us (6%)
  blocking collectives  79.5 us (4%)
  starting transfers between devices  27.1 us (1%)
    reduce_scatter x1, waiting for transfers between devices, reduce_dense(): lax.psum_scatter(qkv_grad, ('dp', 'expert'), scatter_dimension=1, tiled=T...  170 us
    reduce_scatter x1, waiting for transfers between devices, local(): lax.psum_scatter(local_exp_in.astype(jnp.bfloat16), 'dp', scatter_dimensi...  160 us
    all_gather x1, waiting for transfers between devices, local(): lax.all_gather(exp_out.astype(jnp.bfloat16), 'dp', axis=2, tiled=True)  144 us
    reduce_scatter x1, waiting for transfers between devices, reduce_dense(): lax.psum_scatter(down_grad, ('dp', 'expert'), scatter_dimension=1, tiled=...  141 us
    reduce_scatter x1, waiting for transfers between devices, reduce_dense(): lax.psum_scatter(up_grad, ('dp', 'expert'), scatter_dimension=0, tiled=True)  139 us
    reduce_scatter x1, waiting for transfers between devices, local(): lax.psum_scatter(local_exp_out.astype(jnp.bfloat16), 'dp', scatter_dimens...  137 us
    all_gather x1, waiting for transfers between devices, local(): lax.all_gather(exp_in.astype(jnp.bfloat16), 'dp', axis=1, tiled=True)  64.2 us
    dot_general x6, matrix products, matmul_low(): return jnp.dot(left, right, preferred_element_type=jnp.float32)  58.5 us
  transfers between devices with their start and end apart: 21, of which 15 were waited for; matrix products, arithmetic and copies ran while one was open for 20% of the time, Pallas kernels for 0%

profile of v1, /device:TPU:0, one launch (start us, length us, event | category | flops | bytes accessed | tf_op | source)
XLA Modules:
  0.0 1844.5 jit_solution(9562791943161381247)
XLA Ops:
  39.8 15.2 scatter_custom_fusion.1
  67.0 33.4 %collective-permute-done.1 = bf16[4,48]{1,0:T(4,128)(2,1)S(1)} collective-permute-done((bf16[4,48]{1,0:T(4,128)(2,1)S(1)}, bf16[4,48]{1,0:T(4,128)(2,1)S(1)}, u32[]{:S(2)}, u32[]{:S(2)}) %collective-permute-start.1) | collective-permute-done | bytes 416 | tf_op jit(solution)/shard_map/ppermute | solution.py:21
  107.9 42.2 %all-gather = bf16[32,24,4]{1,2,0:T(4,128)(2,1)S(1)} all-gather(bf16[1,24,4]{1,2,0:T(4,128)(2,1)S(1)} %convert_bitcast_fusion), channel_id=1, replica_groups=mesh['dp'=4,'expert'=8] {'dp','expert'}, dimensions={0}, use_global_device_ids=true | all-gather | bytes 6336 | tf_op jit(solution)/shard_map/all_gather | solution.py:59
  156.7 9.2 reshape.362
  201.7 34.5 %all-gather.12.cloned.1.call-done = bf16[768,3072]{1,0:T(8,128)(2,1)} async-done(((bf16[24,3072]{1,0:T(8,128)(2,1)}), bf16[768,3072]{1,0:T(8,128)(2,1)}) %all-gather.12.cloned.1.call-update) | async-done | bytes 4718608 | tf_op jit(solution)/shard_map/all_gather | solution.py:57
  236.3 35.6 %multiply_convert_fusion.3 = (bf16[591,3072]{1,0:T(8,128)(2,1)}, f32[591,3072]{1,0:T(8,128)}, f32[591,3072]{1,0:T(8,128)}) fusion(bf16[768,3072]{1,0:T(8,128)(2,1)} %all-gather.12.cloned.1.call-done, f32[591,768]{1,0:T(8,128)} %copy-done.6, f32[768]{0:T(1024)S(1)} %get-tuple-element.76, f32[768]{0:T(1024)S(1)} %get-tuple-element.119, f32[591]{0:T(1024)S(1)} %fusion.75, ...), kind=kOutput, calls=%fused_computation.39 | convolution fusion | flops 2908968192 | bytes 24700536 | tf_op jit(solution)/shard_map/dot_general | solution.py:50
  271.8 30.2 %all-gather.14.cloned.1.call-done = bf16[3072,768]{0,1:T(8,128)(2,1)} async-done(((bf16[3072,24]{0,1:T(8,128)(2,1)}), bf16[3072,768]{0,1:T(8,128)(2,1)}) %all-gather.14.cloned.1.call-update) | async-done | bytes 4718608 | tf_op jit(solution)/shard_map/all_gather | solution.py:58
  359.8 10.4 scatter_custom_fusion
  377.3 26.1 %all-to-all-done = bf16[16,96,768]{2,1,0:T(8,128)(2,1)S(1)} async-done(((bf16[16,96,768]{2,1,0:T(8,128)(2,1)}), bf16[16,96,768]{2,1,0:T(8,128)(2,1)S(1)}, u32[]{:S(2)}, u32[]{:S(2)}) %all-to-all-start) | async-done | bytes 2359328 | tf_op jit(solution)/shard_map/all_to_all | solution.py:211
  404.9 64.2 %all-gather.16.cloned.1.call-done = bf16[2,768,3072]{2,1,0:T(8,128)(2,1)} async-done(((bf16[2,192,3072]{2,1,0:T(8,128)(2,1)}), bf16[2,768,3072]{2,1,0:T(8,128)(2,1)}) %all-gather.16.cloned.1.call-update) | async-done | bytes 9437200 | tf_op jit(solution)/shard_map/all_gather | solution.py:183
  469.1 22.8 %fusion.17 = (u8[768,3072]{1,0:T(8,128)(4,1)}, u8[768,3072]{1,0:T(8,128)(4,1)}, f32[2,768,3072]{2,1,0:T(8,128)}) fusion(bf16[2,768,768]{2,1,0:T(8,128)(2,1)} %bitcast.193, bf16[2,768,3072]{2,1,0:T(8,128)(2,1)} %all-gather.16.cloned.1.call-done), kind=kOutput, calls=%fused_computation.67 | convolution fusion | flops 7304380416 | bytes 35389440 | tf_op jit(solution)/shard_map/erd,edf->erf/dot_general | solution.py:212
  491.9 143.6 %all-gather.18.cloned.1.call-done = bf16[2,3072,768]{1,2,0:T(8,128)(2,1)} async-done(((bf16[2,3072,192]{1,2,0:T(8,128)(2,1)}), bf16[2,3072,768]{1,2,0:T(8,128)(2,1)}) %all-gather.18.cloned.1.call-update) | async-done | bytes 9437200 | tf_op jit(solution)/shard_map/all_gather | solution.py:184
  635.6 56.1 %add_convert_fusion = (bf16[2,768,3072]{2,1,0:T(8,128)(2,1)}, f32[2,768,3072]{2,1,0:T(8,128)}) fusion(f32[2,768,3072]{2,1,0:T(8,128)} %get-tuple-element.110, u8[768,3072]{1,0:T(8,128)(4,1)} %get-tuple-element.56, u8[768,3072]{1,0:T(8,128)(4,1)} %get-tuple-element.55, bf16[2,768,768]{2,1,0:T(8,128)(2,1)S(1)} %bitcast.196, ...), kind=kOutput, calls=%fused_computation.11 | convolution fusion | flops 7611088896 | bytes 63700992 | tf_op jit(solution)/shard_map/erd,efd->erf/dot_general | solution.py:247
  691.7 13.2 multiply_convert_fusion
  704.9 10.1 convolution_convert_fusion.4
  722.9 12.9 convolution_convert_fusion.5
  739.6 12.7 all-to-all-done.3
  758.9 27.3 %all-to-all-done.1 = bf16[2,768,768]{2,0,1:T(2,128)(2,1)} async-done(((bf16[2,768,768]{2,0,1:T(2,128)(2,1)}), bf16[2,768,768]{2,0,1:T(2,128)(2,1)}, u32[]{:S(2)}, u32[]{:S(2)}) %all-to-all-start.1) | async-done | bytes 2359328 | tf_op jit(solution)/shard_map/all_to_all | solution.py:219
  807.4 10.9 multiply_reduce_fusion.4
  867.4 10.0 convert_element_type.222
  886.5 9.5 add_convert_fusion.1
  914.1 13.8 convolution_convert_fusion
  928.0 14.4 convolution_convert_fusion.1
  991.7 10.1 convert_element_type.230
  1001.8 8.7 convolution_bitcast_fusion
  1016.1 11.3 pad_maximum_fusion
  1037.4 37.3 %all-reduce.4 = (f32[4,768]{1,0:T(4,128)S(1)}, f32[4,768]{1,0:T(4,128)S(1)}) all-reduce(f32[4,768]{1,0:T(4,128)S(1)} %pad_maximum_fusion.2, f32[4,768]{1,0:T(4,128)S(1)} %pad_maximum_fusion.3), channel_id=6, replica_groups=mesh['dp'=4,'expert'=8] {'dp','expert'}, use_global_device_ids=true, to_apply=%region_37.38.clone | all-reduce | flops 6144 | bytes 49152
  1081.3 137.0 %reduce-scatter.16.cloned.1.call-done = bf16[2,3072,192]{1,2,0:T(8,128)(2,1)} async-done(((bf16[2,3072,768]{1,2,0:T(8,128)(2,1)}), bf16[2,3072,192]{1,2,0:T(8,128)(2,1)}) %reduce-scatter.16.cloned.1.call-update) | async-done | bytes 2359312 | tf_op jit(solution)/shard_map/reduce_scatter | solution.py:265
  1222.7 160.2 %reduce-scatter.14.cloned.1.call-done = bf16[2,192,3072]{2,1,0:T(8,128)(2,1)} async-done(((bf16[2,768,3072]{2,1,0:T(8,128)(2,1)}), bf16[2,192,3072]{2,1,0:T(8,128)(2,1)}) %reduce-scatter.14.cloned.1.call-update) | async-done | bytes 2359312 | tf_op jit(solution)/shard_map/reduce_scatter | solution.py:262
  1387.3 139.4 %reduce-scatter.10.cloned.1.call-done = f32[24,3072]{1,0:T(8,128)} async-done(((f32[768,3072]{1,0:T(8,128)}), f32[24,3072]{1,0:T(8,128)}) %reduce-scatter.10.cloned.1.call-update) | async-done | bytes 294928 | tf_op jit(solution)/shard_map/reduce_scatter | solution.py:69
  1526.7 141.0 %reduce-scatter.12.cloned.1.call-done = f32[3072,24]{0,1:T(8,128)} async-done(((f32[3072,768]{0,1:T(8,128)}), f32[3072,24]{0,1:T(8,128)}) %reduce-scatter.12.cloned.1.call-update) | async-done | bytes 294928 | tf_op jit(solution)/shard_map/reduce_scatter | solution.py:70
  1667.7 169.5 %reduce-scatter.8.cloned.1.call-done = f32[2,24,2304]{2,1,0:T(8,128)} async-done(((f32[2,768,2304]{2,1,0:T(8,128)}), f32[2,24,2304]{2,1,0:T(8,128)}) %reduce-scatter.8.cloned.1.call-update) | async-done | bytes 442384 | tf_op jit(solution)/shard_map/reduce_scatter | solution.py:67
  (425 shorter events, 355.5 us)
Async XLA Ops:
  7.2 143.5 %all-gather.8.cloned.1.call-start = ((), (), s32[]{:S(2)}) async-start(), calls=%async_computation.9 | async-start | bytes 7299072 | tf_op jit(solution)/shard_map/all_gather | solution.py:55
  9.0 188.5 %all-gather.10.cloned.1.call-start = ((), (), s32[]{:S(2)}) async-start(), calls=%async_computation.10 | async-start | bytes 2433024 | tf_op jit(solution)/shard_map/all_gather | solution.py:56
  10.6 225.7 %all-gather.12.cloned.1.call-start = ((), (), s32[]{:S(2)}) async-start(), calls=%async_computation.11 | async-start | bytes 4866048 | tf_op jit(solution)/shard_map/all_gather | solution.py:57
  12.3 289.8 %all-gather.14.cloned.1.call-start = ((), (), s32[]{:S(2)}) async-start(), calls=%async_computation.12 | async-start | bytes 4866048 | tf_op jit(solution)/shard_map/all_gather | solution.py:58
  14.1 455.1 %all-gather.16.cloned.1.call-start = ((), (), s32[]{:S(2)}) async-start(), calls=%async_computation.13 | async-start | bytes 11796480 | tf_op jit(solution)/shard_map/all_gather | solution.py:183
  18.2 46.6 %collective-permute-start = (bf16[4,24]{1,0:T(4,128)(2,1)S(1)}, bf16[4,24]{1,0:T(4,128)(2,1)S(1)}, u32[]{:S(2)}, u32[]{:S(2)}) collective-permute-start(bf16[4,24]{1,0:T(4,128)(2,1)S(1)} %convert_element_type.186), channel_id=1, source_target_pairs={{0,31},{1,0},{2,1},{3,2},{4,3},{5,4},{6,5},{7,6},{8,7},{9,8},{10,9... | collective-permute-start | bytes 584 | tf_op jit(solution)/shard_map/ppermute | solution.py:21
  39.8 320.0 %copy-start.84 = (s32[1182]{0:T(1024)}, s32[1182]{0:T(1024)S(1)}, u32[]{:S(2)}) copy-start(s32[1182]{0:T(1024)S(1)} %fusion.73) | copy-start | bytes 14188
  55.0 315.2 %all-to-all-start.2 = ((bf16[16,96,768]{2,1,0:T(8,128)(2,1)}), bf16[16,96,768]{2,1,0:T(8,128)(2,1)}, u32[]{:S(2)}, u32[]{:S(2)}) async-start(bf16[16,96,768]{2,1,0:T(8,128)(2,1)} %bitcast.23), calls=%async_computation.2 | async-start | bytes 4718592 | tf_op jit(solution)/shard_map/all_to_all | solution.py:243
  59.3 576.2 %all-gather.18.cloned.1.call-start = ((), (), s32[]{:S(2)}) async-start(), calls=%async_computation.14 | async-start | bytes 11796480 | tf_op jit(solution)/shard_map/all_gather | solution.py:184
  64.8 91.8 %copy-start.72 = (f32[591]{0:T(1024)}, f32[591]{0:T(1024)S(1)}, u32[]{:S(2)}) copy-start(f32[591]{0:T(1024)S(1)} %broadcast_multiply_fusion.4) | copy-start | bytes 7096
  64.9 35.4 %collective-permute-start.1 = (bf16[4,48]{1,0:T(4,128)(2,1)S(1)}, bf16[4,48]{1,0:T(4,128)(2,1)S(1)}, u32[]{:S(2)}, u32[]{:S(2)}) collective-permute-start(bf16[4,48]{1,0:T(4,128)(2,1)S(1)} %pad_maximum_fusion.5), channel_id=1, source_target_pairs={{0,30},{1,31},{2,0},{3,1},{4,2},{5,3},{6,4},{7,5},{8,6},{9,7},{10,... | collective-permute-start | bytes 1160 | tf_op jit(solution)/shard_map/ppermute | solution.py:21
  100.4 3.6 collective-permute-start.2
  104.1 3.6 collective-permute-start.3
  107.8 42.5 %collective-permute-start.4 = (bf16[4,384]{1,0:T(4,128)(2,1)S(1)}, bf16[4,384]{1,0:T(4,128)(2,1)S(1)}, u32[]{:S(2)}, u32[]{:S(2)}) collective-permute-start(bf16[4,384]{1,0:T(4,128)(2,1)S(1)} %concatenate.25), channel_id=1, source_target_pairs={{0,16},{1,17},{2,18},{3,19},{4,20},{5,21},{6,22},{7,23},{8,24},{9,... | collective-permute-start | bytes 9224 | tf_op jit(solution)/shard_map/ppermute | solution.py:21
  150.6 85.7 %copy-start.56 = (f32[768]{0:T(1024)}, f32[768]{0:T(1024)S(1)}, u32[]{:S(2)}) copy-start(f32[768]{0:T(1024)S(1)} %get-tuple-element.119) | copy-start | bytes 9220
  150.6 85.6 %copy-start.60 = (f32[768]{0:T(1024)}, f32[768]{0:T(1024)S(1)}, u32[]{:S(2)}) copy-start(f32[768]{0:T(1024)S(1)} %get-tuple-element.76) | copy-start | bytes 9220
  150.6 158.4 %copy-start.89 = (f32[768]{0:T(1024)}, f32[768]{0:T(1024)S(1)}, u32[]{:S(2)}) copy-start(f32[768]{0:T(1024)S(1)} %get-tuple-element.120) | copy-start | bytes 9220
  150.6 158.4 %copy-start.99 = (f32[768]{0:T(1024)}, f32[768]{0:T(1024)S(1)}, u32[]{:S(2)}) copy-start(f32[768]{0:T(1024)S(1)} %get-tuple-element.75) | copy-start | bytes 9220
  150.6 203.1 %copy-start.68 = (f32[768]{0:T(1024)}, f32[768]{0:T(1024)S(1)}, u32[]{:S(2)}) copy-start(f32[768]{0:T(1024)S(1)} %get-tuple-element.121) | copy-start | bytes 9220
  200.1 71.7 %copy-start.54 = (f32[591]{0:T(1024)}, f32[591]{0:T(1024)S(1)}, u32[]{:S(2)}) copy-start(f32[591]{0:T(1024)S(1)} %broadcast_multiply_fusion.3) | copy-start | bytes 7096
  201.7 70.1 %copy-start.78 = (f32[591]{0:T(1024)}, f32[591]{0:T(1024)S(1)}, u32[]{:S(2)}) copy-start(f32[591]{0:T(1024)S(1)} %multiply_reduce_fusion.16) | copy-start | bytes 7096
  201.7 70.1 %copy-start.58 = (f32[591]{0:T(1024)}, f32[591]{0:T(1024)S(1)}, u32[]{:S(2)}) copy-start(f32[591]{0:T(1024)S(1)} %fusion.75) | copy-start | bytes 7096
  370.2 33.2 %all-to-all-start = ((bf16[16,96,768]{2,1,0:T(8,128)(2,1)}), bf16[16,96,768]{2,1,0:T(8,128)(2,1)S(1)}, u32[]{:S(2)}, u32[]{:S(2)}) async-start(bf16[16,96,768]{2,1,0:T(8,128)(2,1)} %bitcast.16), calls=%async_computation | async-start | bytes 4718592 | tf_op jit(solution)/shard_map/all_to_all | solution.py:211
  469.1 166.4 %copy-start.48 = (bf16[2,8,96,768]{3,2,1,0:T(8,128)(2,1)S(1)}, bf16[2,8,96,768]{3,2,1,0:T(8,128)(2,1)}, u32[]{:S(2)}) copy-start(bf16[2,8,96,768]{3,2,1,0:T(8,128)(2,1)} %copy.148) | copy-start | bytes 7077892
  718.8 33.5 %all-to-all-start.3 = ((bf16[2,768,768]{2,0,1:T(2,128)(2,1)}), bf16[2,768,768]{2,0,1:T(2,128)(2,1)S(1)}, u32[]{:S(2)}, u32[]{:S(2)}) async-start(bf16[2,768,768]{2,0,1:T(2,128)(2,1)} %copy.149), calls=%async_computation.3 | async-start | bytes 4718592 | tf_op jit(solution)/shard_map/all_to_all | solution.py:257
  752.3 33.9 %all-to-all-start.1 = ((bf16[2,768,768]{2,0,1:T(2,128)(2,1)}), bf16[2,768,768]{2,0,1:T(2,128)(2,1)}, u32[]{:S(2)}, u32[]{:S(2)}) async-start(bf16[2,768,768]{2,0,1:T(2,128)(2,1)} %copy.145), calls=%async_computation.1 | async-start | bytes 4718592 | tf_op jit(solution)/shard_map/all_to_all | solution.py:219
  756.7 323.0 %all-reduce.7.cloned.1.call-start = ((), (), s32[]{:S(2)}) async-start(), calls=%async_computation.20 | async-start | bytes 9437184
  914.1 304.2 %reduce-scatter.16.cloned.1.call-start = ((), (), s32[]{:S(2)}) async-start(), calls=%async_computation.19 | async-start | bytes 11796480 | tf_op jit(solution)/shard_map/reduce_scatter | solution.py:265
  928.0 454.9 %reduce-scatter.14.cloned.1.call-start = ((), (), s32[]{:S(2)}) async-start(), calls=%async_computation.18 | async-start | bytes 11796480 | tf_op jit(solution)/shard_map/reduce_scatter | solution.py:262
  942.5 584.2 %reduce-scatter.10.cloned.1.call-start = ((), (), s32[]{:S(2)}) async-start(), calls=%async_computation.16 | async-start | bytes 9732096 | tf_op jit(solution)/shard_map/reduce_scatter | solution.py:69
  951.8 715.9 %reduce-scatter.12.cloned.1.call-start = ((), (), s32[]{:S(2)}) async-start(), calls=%async_computation.17 | async-start | bytes 9732096 | tf_op jit(solution)/shard_map/reduce_scatter | solution.py:70
  961.5 875.7 %reduce-scatter.8.cloned.1.call-start = ((), (), s32[]{:S(2)}) async-start(), calls=%async_computation.15 | async-start | bytes 14598144 | tf_op jit(solution)/shard_map/reduce_scatter | solution.py:67
  (101 other events, 864.8 us)
Sparse Core Ops, SparseCore 0:
  11.5 91.0 all-gather.7
  106.2 63.9 all-gather.9
  173.7 62.5 all-gather.11
  239.6 62.4 all-gather.13
  303.5 165.5 all-gather.15
  470.5 164.9 all-gather.17
  914.2 141.1 all-reduce.6
  1057.9 160.3 reduce-scatter.15
  1220.8 162.1 reduce-scatter.13
  1390.2 136.4 reduce-scatter.9
  1533.2 134.4 reduce-scatter.11
  1675.1 161.9 reduce-scatter.7
